TPU v7x, 256 devices: a whole 4x4x8 slice. The times are simulated.
256 devices in a mesh: dp: 16 (over y, z_lo, core), own: 16 (over x, z_hi).
Axes of the slice: x: 4, y: 4, z: 8 (z_hi: 4, z_lo: 2; z = z_hi * 2 + z_lo), core: 2. Of those that a mesh axis runs over, the one named last changes fastest.
Arguments:
- grads: bfloat16 [16, 32, 768, 768], P('dp', 'own'), may hold values from -0.059814453 to 0.059814453
- owner: int32 [32], replicated, may hold values from 0 to 15, as said below
- weights: float32 [64, 768, 768], P('own', 'dp'), may hold values from -6 to 6
- stat_left: float32 [64, 768, 768], P('own', 'dp'), may hold values from -3 to 3
- stat_right: float32 [64, 768, 768], P('own', 'dp'), may hold values from -3 to 3
- adam_second: float32 [64, 768, 768], P('own', 'dp'), may hold values from 0.0002 to 1
- root_left: bfloat16 [64, 768, 768], P('own', 'dp'), may hold values from -0.21875 to 0.21875
- root_right: bfloat16 [64, 768, 768], P('own', 'dp'), may hold values from -0.21875 to 0.21875
Outputs:
- new_weights: bfloat16 [64, 768, 768], P('own')
- new_left: float32 [64, 768, 768], P('own', 'dp')
- new_right: float32 [64, 768, 768], P('own', 'dp')
- new_second: float32 [64, 768, 768], P('own', 'dp')
Inputs may be any that keep to these rules, and one draw needn't show every extreme that they name: The 2 blocks 2 * j to 2 * j + 1 have different owners, for every j; one owner holds exactly 4 blocks and none holds more.
All inputs are finite; a program needn't handle non-finite values.
Results may differ from a plain program's by a relative error of at most 0.0095.
Values may be sent and summed in bfloat16 or wider, within the bound.
No kernel may reach another device: no remote copies, remote signals or barrier semaphores. Data moves between devices by JAX's collectives and lax.ppermute only.
A program may use at most 64 MiB of HBM per device.

v0:
```python
import jax
import jax.numpy as jnp
from jax import lax
from jax.sharding import PartitionSpec as P


def slot_index(owner, capacity):
    count = owner.shape[0]
    same = owner[:, None] == owner[None, :]
    earlier = (
        jnp.arange(count, dtype=jnp.int32)[None, :] < jnp.arange(count, dtype=jnp.int32)[:, None]
    )
    rank = jnp.sum((same & earlier).astype(jnp.int32), axis=1)
    return owner * capacity + rank


def on_device(grads, owner, weights, stat_left, stat_right, adam_second, root_left, root_right):
    per_index = grads.shape[1]
    width = grads.shape[3]
    capacity = 2 * per_index
    replicas = lax.axis_size("dp")
    me = lax.axis_index("own")
    rep = lax.axis_index("dp")
    col_count = width // replicas
    summed = lax.psum_scatter(
        grads[0].astype(jnp.float32).astype(jnp.bfloat16), "dp", scatter_dimension=1, tiled=True
    )
    row_count = summed.shape[1]
    slot = slot_index(owner, capacity)
    targets = me * capacity + jnp.arange(capacity, dtype=jnp.int32)
    every = lax.all_gather(summed, "own", axis=0, tiled=True)
    pick = (slot[None, :] == targets[:, None]).astype(jnp.bfloat16)
    mine = jnp.dot(
        pick, every.reshape(every.shape[0], row_count * width), preferred_element_type=jnp.float32
    )
    mine = mine.astype(jnp.bfloat16).reshape(capacity, row_count, width)
    full = lax.all_gather(mine, "dp", axis=1, tiled=True)
    new_left = 0.5 * stat_left + 0.5 * jnp.einsum(
        "srd,sbd->srb", mine, full, preferred_element_type=jnp.float32
    )
    columns = lax.dynamic_slice_in_dim(full, rep * col_count, col_count, 2)
    new_right = 0.5 * stat_right + 0.5 * jnp.einsum(
        "sbc,sbd->scd", columns, full, preferred_element_type=jnp.float32
    )
    grad32 = mine.astype(jnp.float32)
    new_second = 0.9 * adam_second + 0.1 * grad32 * grad32
    adam_dir = grad32 / (jnp.sqrt(new_second) + 1e-08)
    half = jnp.einsum("srb,sbd->srd", root_left, full, preferred_element_type=jnp.float32).astype(
        jnp.bfloat16
    )
    precond = jnp.einsum(
        "src,scd->srd",
        half,
        lax.all_gather(root_right, "dp", axis=1, tiled=True),
        preferred_element_type=jnp.float32,
    )
    adam_sq = jnp.sum(adam_dir * adam_dir, axis=(1, 2))
    prec_sq = jnp.sum(precond * precond, axis=(1, 2))
    adam_total, prec_total = lax.psum((adam_sq, prec_sq), "dp")
    graft = jnp.sqrt(adam_total) / (jnp.sqrt(prec_total) + 1e-06)
    fresh_rows = (weights - graft[:, None, None] * precond).astype(jnp.bfloat16)
    new_weights = lax.all_gather(fresh_rows, "dp", axis=1, tiled=True)
    return (new_weights, new_left, new_right, new_second)


def solution(mesh):
    placed = (
        P("dp", "own", None, None),
        P(),
        P("own", "dp", None),
        P("own", "dp", None),
        P("own", "dp", None),
        P("own", "dp", None),
        P("own", "dp", None),
        P("own", "dp", None),
    )
    return jax.shard_map(
        on_device,
        mesh=mesh,
        in_specs=placed,
        out_specs=(
            P("own", None, None),
            P("own", "dp", None),
            P("own", "dp", None),
            P("own", "dp", None),
        ),
        check_vma=False,
    )
```

profile of v0, /device:TPU:1, one launch (start us, length us, event | category | flops | bytes accessed | tf_op | source)
XLA Modules:
  0.0 314.4 jit_solution(17411451454313605039)
XLA Ops:
  7.2 0.0 copy-start
  7.2 0.0 reduce-scatter.2.cloned.1.call-start
  7.2 0.7 reduce-scatter.2.cloned.1.call-update
  7.9 0.0 copy-start.3
  7.9 0.0 all-gather.5.cloned.1.call-start
  8.0 71.1 %reduce-scatter.2.cloned.1.call-done = bf16[2,48,768]{2,1,0:T(8,128)(2,1)} async-done(((bf16[2,768,768]{2,1,0:T(8,128)(2,1)}), bf16[2,48,768]{2,1,0:T(8,128)(2,1)}) %reduce-scatter.2.cloned.1.call-update) | async-done | bytes 147472 | tf_op jit(solution)/shard_map/reduce_scatter | solution.py:25
  79.1 0.0 all-gather.5.cloned.1.call-update
  79.1 0.0 all-gather.9.cloned.1.call-start
  79.1 0.7 all-gather.9.cloned.1.call-update
  79.8 0.0 all-gather.7.cloned.1.call-start
  79.9 0.9 convert_reduce_fusion
  80.8 0.7 multiply_add_fusion
  81.5 62.1 %all-gather.5.cloned.1.call-done = bf16[32,48,768]{2,1,0:T(8,128)(2,1)} async-done(((bf16[2,48,768]{2,1,0:T(8,128)(2,1)}), bf16[32,48,768]{2,1,0:T(8,128)(2,1)}) %all-gather.5.cloned.1.call-update) | async-done | bytes 2359312 | tf_op jit(solution)/shard_map/all_gather | solution.py:31
  143.5 2.4 copy.16
  146.0 0.5 convolution_convert_fusion
  146.5 0.7 copy.25
  147.2 0.0 all-gather.7.cloned.1.call-update
  147.2 0.0 all-gather.11.cloned.1.call-start
  147.3 0.0 copy-done.3
  147.3 1.1 fusion.6
  148.4 0.0 copy-start.4
  148.4 0.0 copy-start.1
  148.4 36.5 %all-gather.9.cloned.1.call-done = bf16[4,768,768]{2,1,0:T(8,128)(2,1)} async-done(((bf16[4,48,768]{2,1,0:T(8,128)(2,1)}), bf16[4,768,768]{2,1,0:T(8,128)(2,1)}) %all-gather.9.cloned.1.call-update) | async-done | bytes 4718608 | tf_op jit(solution)/shard_map/all_gather | solution.py:54
  185.0 43.2 %all-gather.7.cloned.1.call-done = bf16[4,768,768]{2,1,0:T(8,128)(2,1)} async-done(((bf16[4,48,768]{2,1,0:T(8,128)(2,1)}), bf16[4,768,768]{2,1,0:T(8,128)(2,1)}) %all-gather.7.cloned.1.call-update) | async-done | bytes 4718608 | tf_op jit(solution)/shard_map/all_gather | solution.py:37
  228.2 0.0 copy-done
  228.2 5.6 %multiply_reduce_fusion = (f32[4]{0:T(128)S(1)}, f32[4,48,768]{2,1,0:T(8,128)S(1)}) fusion(bf16[4,768,768]{2,1,0:T(8,128)(2,1)} %all-gather.9.cloned.1.call-done, bf16[4,48,768]{2,1,0:T(8,128)(2,1)S(1)} %copy-done, bf16[4,768,768]{2,1,0:T(8,128)(2,1)} %all-gather.7.cloned.1.call-done), kind=kOutput, calls=%fused_computation.13 | convolution fusion | flops 453427200 | bytes 10321936 | tf_op jit(solution)/shard_map/src,scd->srd/dot_general | solution.py:51
  233.8 26.8 %all-reduce = (f32[4]{0:T(128)S(1)}, f32[4]{0:T(128)S(1)}) all-reduce(f32[4]{0:T(128)S(1)} %get-tuple-element.8, f32[4]{0:T(128)S(1)} %get-tuple-element.6), channel_id=1, replica_groups=mesh['dp'=16,'own'=16] {'dp'}, use_global_device_ids=true, to_apply=%region_5.0 | all-reduce | flops 8 | bytes 64 | tf_op jit(solution)/shard_map/psum | solution.py:59
  260.5 0.0 copy-done.4
  260.5 0.8 subtract_convert_fusion
  261.4 0.0 slice-start
  261.4 0.0 copy-start.2
  261.4 0.0 all-gather.11.cloned.1.call-update
  261.4 0.0 copy-done.1
  261.4 0.0 slice-start.1
  261.4 5.0 %fusion.1 = f32[4,48,768]{2,1,0:T(8,128)} fusion(f32[4,48,768]{2,1,0:T(8,128)S(1)} %copy-done.1, bf16[4,768,768]{2,1,0:T(8,128)(2,1)} %all-gather.7.cloned.1.call-done, s32[]{:T(128)S(6)} %select_n.3), kind=kOutput, calls=%fused_computation.4 | convolution fusion | flops 226787328 | bytes 6684676 | tf_op jit(solution)/shard_map/sbc,sbd->scd/dot_general | solution.py:42
  266.4 0.0 slice-done
  266.4 0.0 copy-done.2
  266.4 0.0 slice-done.1
  266.4 2.3 fusion
  268.7 34.3 %all-gather.11.cloned.1.call-done = bf16[4,768,768]{2,1,0:T(8,128)(2,1)} async-done(((bf16[4,48,768]{2,1,0:T(8,128)(2,1)}), bf16[4,768,768]{2,1,0:T(8,128)(2,1)}) %all-gather.11.cloned.1.call-update) | async-done | bytes 4718608 | tf_op jit(solution)/shard_map/all_gather | solution.py:62
  303.1 4.8 %copy.27 = bf16[4,768,768]{2,1,0:T(8,128)(2,1)} copy(bf16[4,768,768]{2,1,0:T(8,128)(2,1)} %all-gather.11.cloned.1.call-done) | data formatting | bytes 9437184
  (3 shorter events, 0.0 us)
Async XLA Ops:
  7.2 221.0 %copy-start = (bf16[4,48,768]{2,1,0:T(8,128)(2,1)S(1)}, bf16[4,48,768]{2,1,0:T(8,128)(2,1)}, u32[]{:S(2)}) copy-start(bf16[4,48,768]{2,1,0:T(8,128)(2,1)} %param.14) | copy-start | bytes 884740
  7.2 71.9 %reduce-scatter.2.cloned.1.call-start = ((), (), s32[]{:S(2)}) async-start(), calls=%async_computation.1 | async-start | bytes 2506752 | tf_op jit(solution)/shard_map/reduce_scatter | solution.py:25
  7.9 139.4 %copy-start.3 = (f32[4,48,768]{2,1,0:T(8,128)S(1)}, f32[4,48,768]{2,1,0:T(8,128)}, u32[]{:S(2)}) copy-start(f32[4,48,768]{2,1,0:T(8,128)} %param.13) | copy-start | bytes 1769476
  7.9 135.6 %all-gather.5.cloned.1.call-start = ((), (), s32[]{:S(2)}) async-start(), calls=%async_computation.2 | async-start | bytes 2506752 | tf_op jit(solution)/shard_map/all_gather | solution.py:31
  79.1 105.9 %all-gather.9.cloned.1.call-start = ((), (), s32[]{:S(2)}) async-start(), calls=%async_computation.4 | async-start | bytes 5013504 | tf_op jit(solution)/shard_map/all_gather | solution.py:54
  79.8 148.3 %all-gather.7.cloned.1.call-start = ((), (), s32[]{:S(2)}) async-start(), calls=%async_computation.3 | async-start | bytes 5013504 | tf_op jit(solution)/shard_map/all_gather | solution.py:37
  147.2 155.8 %all-gather.11.cloned.1.call-start = ((), (), s32[]{:S(2)}) async-start(), calls=%async_computation.5 | async-start | bytes 5013504 | tf_op jit(solution)/shard_map/all_gather | solution.py:62
  148.4 112.1 %copy-start.4 = (f32[4,48,768]{2,1,0:T(8,128)S(1)}, f32[4,48,768]{2,1,0:T(8,128)}, u32[]{:S(2)}) copy-start(f32[4,48,768]{2,1,0:T(8,128)} %param.10) | copy-start | bytes 1769476
  148.4 113.0 %copy-start.1 = (f32[4,48,768]{2,1,0:T(8,128)S(1)}, f32[4,48,768]{2,1,0:T(8,128)}, u32[]{:S(2)}) copy-start(f32[4,48,768]{2,1,0:T(8,128)} %param.12) | copy-start | bytes 1769476
  261.4 5.0 %slice-start = ((s8[4718592]{0:T(1024)(128)(4,1)}), s8[524288]{0:T(1024)(128)(4,1)S(1)}, s32[]{:S(2)}) async-start(s8[4718592]{0:T(1024)(128)(4,1)} %bitcast.19), calls=%async_computation.6 | async-start | bytes 1048576
  261.4 5.0 %copy-start.2 = (f32[4,48,768]{2,1,0:T(8,128)S(1)}, f32[4,48,768]{2,1,0:T(8,128)}, u32[]{:S(2)}) copy-start(f32[4,48,768]{2,1,0:T(8,128)} %param.11) | copy-start | bytes 1769476
  261.4 5.0 %slice-start.1 = ((s8[4718592]{0:T(1024)(128)(4,1)}), s8[4194304]{0:T(1024)(128)(4,1)S(1)}, s32[]{:S(2)}) async-start(s8[4718592]{0:T(1024)(128)(4,1)} %bitcast.19), calls=%async_computation.7 | async-start | bytes 8388608
Sparse Core Ops, SparseCore 0:
  10.6 68.4 reduce-scatter.1
  81.5 61.9 all-gather.4
  145.3 39.5 all-gather.8
  187.2 40.9 all-gather.6
  261.5 41.4 all-gather.10
where the time goes:
time: 315 us; the launch traced here: 314 us
  waiting for transfers between devices  249 us (79%)
  blocking collectives  26.8 us (9%)
  between operations  13.9 us (4%)
  matrix products  13.4 us (4%)
  local copies, waits for them, and re-layouts  8.03 us (3%)
  other arithmetic  3.58 us (1%)
    reduce_scatter x1, waiting for transfers between devices, on_device(): lax.psum_scatter(grads[0].astype(jnp.float32).astype(jnp.bfloat16), 'dp',...  71.1 us
    all_gather x1, waiting for transfers between devices, on_device(): every = lax.all_gather(summed, 'own', axis=0, tiled=True)  62.1 us
    all_gather x1, waiting for transfers between devices, on_device(): full = lax.all_gather(mine, 'dp', axis=1, tiled=True)  43.2 us
    all_gather x1, waiting for transfers between devices, on_device(): lax.all_gather(root_right, 'dp', axis=1, tiled=True)  36.5 us
    all_gather x1, waiting for transfers between devices, on_device(): new_weights = lax.all_gather(fresh_rows, 'dp', axis=1, tiled=True)  34.3 us
    psum x1, blocking collectives, on_device(): adam_total, prec_total = lax.psum((adam_sq, prec_sq), 'dp')  26.8 us
    unnamed x17, local copies, waits for them, and re-layouts  8.03 us
  transfers between devices with their start and end apart: 5, of which 5 were waited for; matrix products, arithmetic and copies ran while one was open for 4% of the time, Pallas kernels for 0%

commit v1 on v0

--- a/solution.py
+++ b/solution.py
@@ -2,6 +2,11 @@
 import jax.numpy as jnp
 from jax import lax
 from jax.sharding import PartitionSpec as P
+
+
+def gather_over(value, name, d):
+    sent = jnp.stack([value] * lax.axis_size(name))
+    return jnp.concatenate(lax.all_to_all(sent, name, 0, 0), axis=d)
 
 
 def slot_index(owner, capacity):
@@ -49,10 +54,7 @@
         jnp.bfloat16
     )
     precond = jnp.einsum(
-        "src,scd->srd",
-        half,
-        lax.all_gather(root_right, "dp", axis=1, tiled=True),
-        preferred_element_type=jnp.float32,
+        "src,scd->srd", half, gather_over(root_right, "dp", 1), preferred_element_type=jnp.float32
     )
     adam_sq = jnp.sum(adam_dir * adam_dir, axis=(1, 2))
     prec_sq = jnp.sum(precond * precond, axis=(1, 2))

time: 315 us -> 284 us (0.902)
  waiting for transfers between devices: 249 us -> 203 us
  local copies, waits for them, and re-layouts: 8.03 us -> 16.7 us
  starting transfers between devices: 0.19 us -> 8.2 us
    all_gather x1 -> x0, waiting for transfers between devices: 36.5 us -> none  [on_device(): lax.all_gather(root_right, 'dp', axis=1, tiled=True)]
    all_gather x1, waiting for transfers between devices: 43.2 us -> 21.1 us  [on_device(): full = lax.all_gather(mine, 'dp', axis=1, tiled=True)]
    all_to_all x0 -> x1, waiting for transfers between devices: none -> 11.9 us  [gather_over(): return jnp.concatenate(lax.all_to_all(sent, name, 0, 0), axis=d)]
    all_to_all x0 -> x1, starting transfers between devices: none -> 8.04 us  [gather_over(): return jnp.concatenate(lax.all_to_all(sent, name, 0, 0), axis=d)]
    reshape x0 -> x1, local copies, waits for them, and re-layouts: none -> 5.05 us  [gather_over(): return jnp.concatenate(lax.all_to_all(sent, name, 0, 0), axis=d)]
    another operation x0 -> x1, local copies, waits for them, and re-layouts: none -> 3.61 us  [gather_over(): sent = jnp.stack([value] * lax.axis_size(name))]
    unnamed x17 -> x19, local copies, waits for them, and re-layouts: 8.03 us -> 8.04 us
  transfers between devices with their start and end apart: 5 -> 5, of which waited for: 5 -> 5; matrix products, arithmetic and copies ran while one was open for 4% -> 7% of each run, Pallas kernels for 0% -> 0%
where the time goes in v1:
time: 284 us
  waiting for transfers between devices  203 us (71%)
  blocking collectives  26.8 us (9%)
  local copies, waits for them, and re-layouts  16.7 us (6%)
  between operations  13.8 us (5%)
  matrix products  13.4 us (5%)
  starting transfers between devices  8.2 us (3%)
    reduce_scatter x1, waiting for transfers between devices, on_device(): lax.psum_scatter(grads[0].astype(jnp.float32).astype(jnp.bfloat16), 'dp',...  71.1 us
    all_gather x1, waiting for transfers between devices, on_device(): every = lax.all_gather(summed, 'own', axis=0, tiled=True)  63.4 us
    all_gather x1, waiting for transfers between devices, on_device(): new_weights = lax.all_gather(fresh_rows, 'dp', axis=1, tiled=True)  34.3 us
    psum x1, blocking collectives, on_device(): adam_total, prec_total = lax.psum((adam_sq, prec_sq), 'dp')  26.8 us
    all_gather x1, waiting for transfers between devices, on_device(): full = lax.all_gather(mine, 'dp', axis=1, tiled=True)  21.1 us
    all_to_all x1, waiting for transfers between devices, gather_over(): return jnp.concatenate(lax.all_to_all(sent, name, 0, 0), axis=d)  11.9 us
    all_to_all x1, starting transfers between devices, gather_over(): return jnp.concatenate(lax.all_to_all(sent, name, 0, 0), axis=d)  8.04 us
    unnamed x19, local copies, waits for them, and re-layouts  8.04 us
  transfers between devices with their start and end apart: 5, of which 5 were waited for; matrix products, arithmetic and copies ran while one was open for 7% of the time, Pallas kernels for 0%

profile of v1, /device:TPU:1, one launch (start us, length us, event | category | flops | bytes accessed | tf_op | source)
XLA Modules:
  0.0 283.7 jit_solution(17649928235604727082)
XLA Ops:
  7.2 0.0 copy-start
  7.2 0.0 reduce-scatter.2.cloned.1.call-start
  7.2 0.7 reduce-scatter.2.cloned.1.call-update
  7.9 0.0 all-gather.4.cloned.1.call-start
  8.0 71.1 %reduce-scatter.2.cloned.1.call-done = bf16[2,48,768]{2,1,0:T(8,128)(2,1)} async-done(((bf16[2,768,768]{2,1,0:T(8,128)(2,1)}), bf16[2,48,768]{2,1,0:T(8,128)(2,1)}) %reduce-scatter.2.cloned.1.call-update) | async-done | bytes 147472 | tf_op jit(solution)/shard_map/reduce_scatter | solution.py:30
  79.1 0.0 all-gather.4.cloned.1.call-update
  79.1 3.6 %stack.2 = bf16[16,4,48,768]{3,2,1,0:T(8,128)(2,1)} broadcast(bf16[4,48,768]{2,1,0:T(8,128)(2,1)} %param.15), dimensions={1,2,3} | broadcast | bytes 5013504 | tf_op jit(solution)/shard_map/stack | solution.py:8
  82.7 0.0 copy-start.5
  82.7 8.0 %all-to-all-start = ((bf16[16,4,48,768]{3,2,1,0:T(8,128)(2,1)}), bf16[16,4,48,768]{3,2,1,0:T(8,128)(2,1)}, u32[]{:S(2)}, u32[]{:S(2)}) async-start(bf16[16,4,48,768]{3,2,1,0:T(8,128)(2,1)} %stack.2), calls=%async_computation.1 | async-start | bytes 9437184 | tf_op jit(solution)/shard_map/all_to_all | solution.py:9
  90.7 0.0 all-gather.6.cloned.1.call-start
  90.8 0.0 copy-done.5
  90.8 0.2 convert_reduce_fusion
  91.0 63.4 %all-gather.4.cloned.1.call-done = bf16[32,48,768]{2,1,0:T(8,128)(2,1)} async-done(((bf16[2,48,768]{2,1,0:T(8,128)(2,1)}), bf16[32,48,768]{2,1,0:T(8,128)(2,1)}) %all-gather.4.cloned.1.call-update) | async-done | bytes 2359312 | tf_op jit(solution)/shard_map/all_gather | solution.py:36
  154.4 2.4 copy.18
  156.8 0.5 convolution_convert_fusion
  157.3 0.7 copy.27
  158.1 0.0 all-gather.6.cloned.1.call-update
  158.1 0.0 all-gather.8.cloned.1.call-start
  158.1 11.9 %all-to-all-done = bf16[16,4,48,768]{3,2,1,0:T(8,128)(2,1)} async-done(((bf16[16,4,48,768]{3,2,1,0:T(8,128)(2,1)}), bf16[16,4,48,768]{3,2,1,0:T(8,128)(2,1)}, u32[]{:S(2)}, u32[]{:S(2)}) %all-to-all-start) | async-done | bytes 4718624 | tf_op jit(solution)/shard_map/all_to_all | solution.py:9
  170.1 0.0 copy-start.3
  170.1 5.1 %copy.15 = bf16[4,16,48,768]{3,2,1,0:T(8,128)(2,1)} copy(bf16[4,16,48,768]{3,2,0,1:T(8,128)(2,1)} %bitcast.1) | data formatting | bytes 9437184 | tf_op jit(solution)/shard_map/reshape | solution.py:9
  175.1 0.0 copy-done.3
  175.1 1.1 fusion.6
  176.3 21.1 %all-gather.6.cloned.1.call-done = bf16[4,768,768]{2,1,0:T(8,128)(2,1)} async-done(((bf16[4,48,768]{2,1,0:T(8,128)(2,1)}), bf16[4,768,768]{2,1,0:T(8,128)(2,1)}) %all-gather.6.cloned.1.call-update) | async-done | bytes 4718608 | tf_op jit(solution)/shard_map/all_gather | solution.py:42
  197.4 0.0 copy-done
  197.4 0.0 copy-start.4
  197.4 0.0 copy-start.1
  197.4 5.7 %multiply_reduce_fusion = (f32[4]{0:T(128)S(1)}, f32[4,48,768]{2,1,0:T(8,128)S(1)}) fusion(bf16[4,768,768]{2,1,0:T(8,128)(2,1)} %bitcast.23, bf16[4,48,768]{2,1,0:T(8,128)(2,1)S(1)} %copy-done, bf16[4,768,768]{2,1,0:T(8,128)(2,1)} %all-gather.6.cloned.1.call-done), kind=kOutput, calls=%fused_computation.13 | convolution fusion | flops 453427200 | bytes 10321936 | tf_op jit(solution)/shard_map/src,scd->srd/dot_general | solution.py:56
  203.1 26.8 %all-reduce = (f32[4]{0:T(128)S(1)}, f32[4]{0:T(128)S(1)}) all-reduce(f32[4]{0:T(128)S(1)} %get-tuple-element.8, f32[4]{0:T(128)S(1)} %get-tuple-element.6), channel_id=1, replica_groups=mesh['dp'=16,'own'=16] {'dp'}, use_global_device_ids=true, to_apply=%region_5.0 | all-reduce | flops 8 | bytes 64 | tf_op jit(solution)/shard_map/psum | solution.py:61
  229.9 0.0 copy-done.4
  229.9 0.8 subtract_convert_fusion
  230.7 0.0 slice-start
  230.7 0.0 copy-start.2
  230.7 0.0 all-gather.8.cloned.1.call-update
  230.7 0.0 copy-done.1
  230.8 0.0 slice-start.1
  230.8 5.0 %fusion.1 = f32[4,48,768]{2,1,0:T(8,128)} fusion(f32[4,48,768]{2,1,0:T(8,128)S(1)} %copy-done.1, bf16[4,768,768]{2,1,0:T(8,128)(2,1)} %all-gather.6.cloned.1.call-done, s32[]{:T(128)S(6)} %select_n.3), kind=kOutput, calls=%fused_computation.4 | convolution fusion | flops 226787328 | bytes 6684676 | tf_op jit(solution)/shard_map/sbc,sbd->scd/dot_general | solution.py:47
  235.7 0.0 slice-done
  235.7 0.0 copy-done.2
  235.7 0.0 slice-done.1
  235.8 2.3 fusion
  238.1 34.3 %all-gather.8.cloned.1.call-done = bf16[4,768,768]{2,1,0:T(8,128)(2,1)} async-done(((bf16[4,48,768]{2,1,0:T(8,128)(2,1)}), bf16[4,768,768]{2,1,0:T(8,128)(2,1)}) %all-gather.8.cloned.1.call-update) | async-done | bytes 4718608 | tf_op jit(solution)/shard_map/all_gather | solution.py:64
  272.3 4.8 %copy.29 = bf16[4,768,768]{2,1,0:T(8,128)(2,1)} copy(bf16[4,768,768]{2,1,0:T(8,128)(2,1)} %all-gather.8.cloned.1.call-done) | data formatting | bytes 9437184
  (4 shorter events, 0.0 us)
Async XLA Ops:
  7.2 190.2 %copy-start = (bf16[4,48,768]{2,1,0:T(8,128)(2,1)S(1)}, bf16[4,48,768]{2,1,0:T(8,128)(2,1)}, u32[]{:S(2)}) copy-start(bf16[4,48,768]{2,1,0:T(8,128)(2,1)} %param.14) | copy-start | bytes 884740
  7.2 71.9 %reduce-scatter.2.cloned.1.call-start = ((), (), s32[]{:S(2)}) async-start(), calls=%async_computation.2 | async-start | bytes 2506752 | tf_op jit(solution)/shard_map/reduce_scatter | solution.py:30
  7.9 146.5 %all-gather.4.cloned.1.call-start = ((), (), s32[]{:S(2)}) async-start(), calls=%async_computation.3 | async-start | bytes 2506752 | tf_op jit(solution)/shard_map/all_gather | solution.py:36
  82.7 8.1 %copy-start.5 = (s32[32]{0:T(128)S(1)}, s32[32]{0:T(128)}, u32[]{:S(2)}) copy-start(s32[32]{0:T(128)} %param.9) | copy-start | bytes 388
  82.7 87.4 %all-to-all-start = ((bf16[16,4,48,768]{3,2,1,0:T(8,128)(2,1)}), bf16[16,4,48,768]{3,2,1,0:T(8,128)(2,1)}, u32[]{:S(2)}, u32[]{:S(2)}) async-start(bf16[16,4,48,768]{3,2,1,0:T(8,128)(2,1)} %stack.2), calls=%async_computation.1 | async-start | bytes 9437184 | tf_op jit(solution)/shard_map/all_to_all | solution.py:9
  90.7 106.6 %all-gather.6.cloned.1.call-start = ((), (), s32[]{:S(2)}) async-start(), calls=%async_computation.4 | async-start | bytes 5013504 | tf_op jit(solution)/shard_map/all_gather | solution.py:42
  158.1 114.2 %all-gather.8.cloned.1.call-start = ((), (), s32[]{:S(2)}) async-start(), calls=%async_computation.5 | async-start | bytes 5013504 | tf_op jit(solution)/shard_map/all_gather | solution.py:64
  170.1 5.1 %copy-start.3 = (f32[4,48,768]{2,1,0:T(8,128)S(1)}, f32[4,48,768]{2,1,0:T(8,128)}, u32[]{:S(2)}) copy-start(f32[4,48,768]{2,1,0:T(8,128)} %param.13) | copy-start | bytes 1769476
  197.4 32.5 %copy-start.4 = (f32[4,48,768]{2,1,0:T(8,128)S(1)}, f32[4,48,768]{2,1,0:T(8,128)}, u32[]{:S(2)}) copy-start(f32[4,48,768]{2,1,0:T(8,128)} %param.10) | copy-start | bytes 1769476
  197.4 33.4 %copy-start.1 = (f32[4,48,768]{2,1,0:T(8,128)S(1)}, f32[4,48,768]{2,1,0:T(8,128)}, u32[]{:S(2)}) copy-start(f32[4,48,768]{2,1,0:T(8,128)} %param.12) | copy-start | bytes 1769476
  230.7 5.0 %slice-start = ((s8[4718592]{0:T(1024)(128)(4,1)}), s8[524288]{0:T(1024)(128)(4,1)S(1)}, s32[]{:S(2)}) async-start(s8[4718592]{0:T(1024)(128)(4,1)} %bitcast.21), calls=%async_computation.6 | async-start | bytes 1048576
  230.7 5.0 %copy-start.2 = (f32[4,48,768]{2,1,0:T(8,128)S(1)}, f32[4,48,768]{2,1,0:T(8,128)}, u32[]{:S(2)}) copy-start(f32[4,48,768]{2,1,0:T(8,128)} %param.11) | copy-start | bytes 1769476
  230.8 5.0 %slice-start.1 = ((s8[4718592]{0:T(1024)(128)(4,1)}), s8[4194304]{0:T(1024)(128)(4,1)S(1)}, s32[]{:S(2)}) async-start(s8[4718592]{0:T(1024)(128)(4,1)} %bitcast.21), calls=%async_computation.7 | async-start | bytes 8388608
Sparse Core Ops, SparseCore 0:
  10.6 68.4 reduce-scatter.1
  81.5 72.8 all-gather.3
  158.2 39.1 all-gather.5
  230.9 41.4 all-gather.7
